TPU v7x, 32 devices: a whole 2x2x4 slice. The times are simulated.
32 devices in a mesh: patch: 16 (over z, y, x), rep: 2 (over core).
Axes of the slice: x: 2, y: 2, z: 4, core: 2. Of those that a mesh axis runs over, the one named last changes fastest.
Arguments:
- tokens: bfloat16 [8192, 512], P(('patch', 'rep')), may hold values from -6 to 6
- cotangent: bfloat16 [8192, 512], P(('patch', 'rep')), may hold values from -6 to 6
- dest: int32 [8192], P(('patch', 'rep')), may hold values from 0 to 15, as said below
- neighbours: int32 [8192, 16], P(('patch', 'rep')), may hold values from 0 to 8191, as said below
- w_qkv: bfloat16 [512, 1536], replicated, may hold values from -0.25 to 0.25
- w_out: bfloat16 [512, 512], replicated, may hold values from -1 to 1
- w_up: bfloat16 [512, 2048], replicated, may hold values from -0.25 to 0.25
- w_down: bfloat16 [2048, 512], replicated, may hold values from -0.125 to 0.125
- ada_attn: float32 [32, 1024], replicated, may hold values from -0.5 to 0.5
- ada_mlp: float32 [32, 1024], replicated, may hold values from -0.5 to 0.5
- cond: float32 [32], replicated, may hold values from -4 to 4
Outputs:
- output: bfloat16 [8192, 512], P(('patch', 'rep'))
- grad_tokens: bfloat16 [8192, 512], P(('patch', 'rep'))
- grad_qkv: float32 [512, 1536], replicated
- grad_out: float32 [512, 512], replicated
- grad_up: float32 [512, 2048], replicated
- grad_down: float32 [2048, 512], replicated
- grad_ada_attn: float32 [32, 1024], replicated
- grad_ada_mlp: float32 [32, 1024], replicated
- grad_cond: float32 [32], replicated
Inputs may be any that keep to these rules, and one draw needn't show every extreme that they name: `dest`: within each index of rep, every patch receives exactly 256 rows; one device sends at most 17 rows to one patch, and each device sends exactly 17 rows to some patch. neighbours[i, 0] = i; every other neighbour of a node in patch q lies in the rows of the same index of rep in patch q - 1, q or q + 1, counted cyclically over 16 patches; positions may repeat.
All inputs are finite; a program needn't handle non-finite values.
Results may differ from a plain program's by a relative error of at most 0.013.
Values may be sent and summed in bfloat16 or wider, within the bound.
A program may use at most 128 MiB of HBM per device.

v0:
```python
import jax
import jax.numpy as jnp
from jax import lax
from jax.sharding import PartitionSpec as P

H = 4
HD = 128
NEIGH = 16
NORM_EPS = 1e-05


def extended(cells, sides, width):
    for axis, dim in sides:
        count = lax.axis_size(axis)
        head = lax.slice_in_dim(cells, 0, width, axis=dim)
        tail = lax.slice_in_dim(cells, cells.shape[dim] - width, cells.shape[dim], axis=dim)
        cells = jnp.concatenate(
            [
                lax.ppermute(tail, axis, [(i, (i + 1) % count) for i in range(count)]),
                cells,
                lax.ppermute(head, axis, [((i + 1) % count, i) for i in range(count)]),
            ],
            axis=dim,
        )
    return cells


def from_behind(array, axis, by):
    size = lax.axis_size(axis)
    return lax.ppermute(array, axis, [(i, (i + by) % size) for i in range(size)])


def norm_parts(values_in):
    centre = jnp.mean(values_in, axis=-1, keepdims=True)
    centred = values_in - centre
    inverse = lax.rsqrt(jnp.mean(centred * centred, axis=-1, keepdims=True) + NORM_EPS)
    return (centred * inverse, inverse)


def norm_back(grad_normed, plain, inverse, coeffs):
    feature_width = plain.shape[-1]
    scaled = grad_normed * (1.0 + coeffs[:feature_width])
    inner = (
        scaled
        - jnp.mean(scaled, axis=-1, keepdims=True)
        - plain * jnp.mean(scaled * plain, axis=-1, keepdims=True)
    )
    coeff_grad = jnp.concatenate(
        [jnp.sum(grad_normed * plain, axis=0), jnp.sum(grad_normed, axis=0)]
    )
    return (inverse * inner, coeff_grad)


def local(tokens, cotangent, dest, neighbours, w_qkv, w_out, w_up, w_down, ada_attn, ada_mlp, cond):
    highest = lax.Precision.HIGHEST
    row_count = tokens.shape[0]
    feature_width = tokens.shape[1]
    patch_count = lax.axis_size("patch")
    group_count = lax.axis_size("rep")
    capacity = row_count // patch_count + 1
    one_hot = (dest[:, None] == jnp.arange(patch_count, dtype=jnp.int32)[None, :]).astype(jnp.int32)
    earlier = jnp.cumsum(one_hot, axis=0) - one_hot
    slot_index = jnp.sum(earlier * one_hot, axis=1)
    sent_counts = jnp.sum(one_hot, axis=0)
    flat_slot = dest * capacity + slot_index
    outgoing = jnp.zeros((patch_count * capacity, 2 * feature_width), jnp.bfloat16)
    outgoing = outgoing.at[flat_slot].set(jnp.concatenate([tokens, cotangent], axis=1))
    arrived, arrived_counts = (
        lax.all_to_all(
            outgoing.reshape(patch_count, capacity, 2 * feature_width),
            "patch",
            split_axis=0,
            concat_axis=0,
            tiled=True,
        ),
        lax.all_to_all(sent_counts[:, None], "patch", split_axis=0, concat_axis=0, tiled=True),
    )
    counts_in = arrived_counts[:, 0]
    offsets = jnp.cumsum(counts_in) - counts_in
    columns = jnp.arange(capacity, dtype=jnp.int32)
    target = jnp.where(
        columns[None, :] < counts_in[:, None], offsets[:, None] + columns[None, :], row_count
    ).reshape(-1)
    placed = (
        jnp.zeros((row_count + 1, 2 * feature_width), jnp.bfloat16)
        .at[target]
        .set(arrived.reshape(-1, 2 * feature_width))[:row_count]
    )
    node_rows = placed[:, :feature_width].astype(jnp.float32)
    upstream = placed[:, feature_width:]
    coeff_attn = jnp.dot(cond, ada_attn, precision=highest)
    coeff_mlp = jnp.dot(cond, ada_mlp, precision=highest)
    plain_first, inv_first = norm_parts(node_rows)
    normed = (plain_first * (1.0 + coeff_attn[:feature_width]) + coeff_attn[feature_width:]).astype(
        jnp.bfloat16
    )
    projected = jnp.dot(normed, w_qkv, preferred_element_type=jnp.float32)
    queries = projected[:, :feature_width].astype(jnp.bfloat16)
    key_value = projected[:, feature_width:].astype(jnp.bfloat16)
    beside_all = extended(normed, (("patch", 0),), row_count)
    side_rows = jnp.concatenate([beside_all[:row_count], beside_all[2 * row_count :]], axis=0)
    side_kv = jnp.dot(
        side_rows, w_qkv[:, feature_width:], preferred_element_type=jnp.float32
    ).astype(jnp.bfloat16)
    kv_table = jnp.concatenate([side_kv[:row_count], key_value, side_kv[row_count:]], axis=0)
    my_patch = lax.axis_index("patch")
    owners = neighbours // row_count // group_count
    local_row = neighbours % row_count
    rel_patch = (owners - my_patch) % patch_count
    table_index = jnp.where(
        rel_patch == 0,
        row_count + local_row,
        jnp.where(rel_patch == 1, 2 * row_count + local_row, local_row),
    )
    block_rows = min(512, row_count)
    block_count = row_count // block_rows
    score_scale = 1.0 / HD**0.5

    def gather_block(index_block):
        gathered = kv_table[index_block]
        key_block = gathered[..., :feature_width].reshape(block_rows, NEIGH, H, HD)
        value_block = gathered[..., feature_width:].reshape(block_rows, NEIGH, H, HD)
        return (key_block, value_block)

    def forward_block(pieces):
        query_block, index_block = pieces
        key_block, value_block = gather_block(index_block)
        scores = (
            jnp.einsum(
                "bhd,bjhd->bhj",
                query_block.reshape(block_rows, H, HD),
                key_block,
                preferred_element_type=jnp.float32,
            )
            * score_scale
        )
        row_max = jnp.max(scores, axis=-1, keepdims=True)
        row_total = jnp.sum(jnp.exp(scores - row_max), axis=-1, keepdims=True)
        log_total = row_max + jnp.log(row_total)
        weights = jnp.exp(scores - log_total).astype(jnp.bfloat16)
        mixture = jnp.einsum(
            "bhj,bjhd->bhd", weights, value_block, preferred_element_type=jnp.float32
        )
        return (mixture.reshape(block_rows, feature_width).astype(jnp.bfloat16), log_total[..., 0])

    query_blocks = queries.reshape(block_count, block_rows, feature_width)
    index_blocks = table_index.reshape(block_count, block_rows, NEIGH)
    heads_out, log_totals = lax.map(forward_block, (query_blocks, index_blocks))
    heads_out = heads_out.reshape(row_count, feature_width)
    residual = node_rows + jnp.dot(heads_out, w_out, preferred_element_type=jnp.float32)
    plain_second, inv_second = norm_parts(residual)
    normed_mlp = (
        plain_second * (1.0 + coeff_mlp[:feature_width]) + coeff_mlp[feature_width:]
    ).astype(jnp.bfloat16)
    up_proj = jnp.dot(normed_mlp, w_up, preferred_element_type=jnp.float32)
    activation = jax.nn.silu(up_proj).astype(jnp.bfloat16)
    output_rows = residual + jnp.dot(activation, w_down, preferred_element_type=jnp.float32)
    gradient_down = jnp.einsum(
        "ri,rj->ij", activation, upstream, preferred_element_type=jnp.float32
    )
    grad_act = jnp.einsum("rj,ij->ri", upstream, w_down, preferred_element_type=jnp.float32)
    sigmoid_up = jax.nn.sigmoid(up_proj)
    grad_upproj = (grad_act * sigmoid_up * (1.0 + up_proj * (1.0 - sigmoid_up))).astype(
        jnp.bfloat16
    )
    gradient_up = jnp.einsum(
        "ri,rj->ij", normed_mlp, grad_upproj, preferred_element_type=jnp.float32
    )
    grad_normed_mlp = jnp.einsum("rj,ij->ri", grad_upproj, w_up, preferred_element_type=jnp.float32)
    grad_resid_norm, coeff_mlp_grad = norm_back(
        grad_normed_mlp, plain_second, inv_second, coeff_mlp
    )
    grad_residual = upstream.astype(jnp.float32) + grad_resid_norm
    grad_branch = grad_residual.astype(jnp.bfloat16)
    gradient_out = jnp.einsum(
        "ri,rj->ij", heads_out, grad_branch, preferred_element_type=jnp.float32
    )
    grad_heads = jnp.einsum(
        "rj,ij->ri", grad_branch, w_out, preferred_element_type=jnp.float32
    ).astype(jnp.bfloat16)

    def backward_block(table_grad, pieces):
        query_block, index_block, log_block, heads_grad = pieces
        key_block, value_block = gather_block(index_block)
        query_heads = query_block.reshape(block_rows, H, HD)
        scores = (
            jnp.einsum("bhd,bjhd->bhj", query_heads, key_block, preferred_element_type=jnp.float32)
            * score_scale
        )
        weights = jnp.exp(scores - log_block[..., None])
        weights_low = weights.astype(jnp.bfloat16)
        grad_heads_block = heads_grad.reshape(block_rows, H, HD)
        grad_weights = jnp.einsum(
            "bhd,bjhd->bhj", grad_heads_block, value_block, preferred_element_type=jnp.float32
        )
        grad_scores = weights * (
            grad_weights - jnp.sum(weights * grad_weights, axis=-1, keepdims=True)
        )
        scores_low = grad_scores.astype(jnp.bfloat16)
        grad_query = (
            jnp.einsum("bhj,bjhd->bhd", scores_low, key_block, preferred_element_type=jnp.float32)
            * score_scale
        )
        grad_key = (
            jnp.einsum("bhj,bhd->bjhd", scores_low, query_heads, preferred_element_type=jnp.float32)
            * score_scale
        )
        grad_value = jnp.einsum(
            "bhj,bhd->bjhd", weights_low, grad_heads_block, preferred_element_type=jnp.float32
        )
        pair_grad = jnp.concatenate(
            [
                grad_key.reshape(block_rows * NEIGH, feature_width),
                grad_value.reshape(block_rows * NEIGH, feature_width),
            ],
            axis=1,
        )
        table_grad = table_grad.at[index_block.reshape(-1)].add(pair_grad)
        return (table_grad, grad_query.reshape(block_rows, feature_width))

    table_grad, grad_queries = lax.scan(
        backward_block,
        jnp.zeros((3 * row_count, 2 * feature_width), jnp.float32),
        (
            query_blocks,
            index_blocks,
            log_totals,
            grad_heads.reshape(block_count, block_rows, feature_width),
        ),
    )
    returned = table_grad[row_count : 2 * row_count]
    for shift_by, side_piece in ((-1, table_grad[:row_count]), (1, table_grad[2 * row_count :])):
        returned = returned + from_behind(
            side_piece.astype(jnp.bfloat16), "patch", shift_by
        ).astype(side_piece.dtype)
    grad_projected = jnp.concatenate(
        [grad_queries.reshape(row_count, feature_width), returned], axis=1
    ).astype(jnp.bfloat16)
    gradient_proj = jnp.einsum(
        "ri,rj->ij", normed, grad_projected, preferred_element_type=jnp.float32
    )
    grad_normed = jnp.einsum("rj,ij->ri", grad_projected, w_qkv, preferred_element_type=jnp.float32)
    grad_input_norm, coeff_attn_grad = norm_back(grad_normed, plain_first, inv_first, coeff_attn)
    grad_input = (grad_residual + grad_input_norm).astype(jnp.bfloat16)
    gradient_proj, gradient_out, gradient_up, gradient_down, coeff_attn_grad, coeff_mlp_grad = (
        lax.psum(
            (
                gradient_proj,
                gradient_out,
                gradient_up,
                gradient_down,
                coeff_attn_grad,
                coeff_mlp_grad,
            ),
            ("patch", "rep"),
        )
    )
    gradient_ada_attn = jnp.outer(cond, coeff_attn_grad)
    gradient_ada_mlp = jnp.outer(cond, coeff_mlp_grad)
    gradient_cond = jnp.dot(ada_attn, coeff_attn_grad, precision=highest) + jnp.dot(
        ada_mlp, coeff_mlp_grad, precision=highest
    )
    leaving = jnp.concatenate([output_rows.astype(jnp.bfloat16), grad_input], axis=1)
    padded = jnp.concatenate([leaving, jnp.zeros((1, 2 * feature_width), jnp.bfloat16)], axis=0)
    going_back = padded[target].reshape(patch_count, capacity, 2 * feature_width)
    home_rows = lax.all_to_all(
        going_back, "patch", split_axis=0, concat_axis=0, tiled=True
    ).reshape(-1, 2 * feature_width)
    band_rows = home_rows[flat_slot]
    return (
        band_rows[:, :feature_width],
        band_rows[:, feature_width:],
        gradient_proj,
        gradient_out,
        gradient_up,
        gradient_down,
        gradient_ada_attn,
        gradient_ada_mlp,
        gradient_cond,
    )


def solution(mesh):
    return jax.shard_map(
        local,
        mesh=mesh,
        in_specs=(
            P(("patch", "rep"), None),
            P(("patch", "rep"), None),
            P(("patch", "rep")),
            P(("patch", "rep"), None),
            P(),
            P(),
            P(),
            P(),
            P(),
            P(),
            P(),
        ),
        out_specs=(
            P(("patch", "rep"), None),
            P(("patch", "rep"), None),
            P(),
            P(),
            P(),
            P(),
            P(),
            P(),
            P(),
        ),
        check_vma=False,
    )
```

profile of v0, /device:TPU:0, one launch (start us, length us, event | category | flops | bytes accessed | tf_op | source)
XLA Modules:
  0.0 489.2 jit_solution(324026931602704912)
XLA Ops:
  7.2 0.8 fusion.79
  8.9 0.9 fusion.74
  10.4 8.3 %all-to-all-start = ((s32[16,1,1]{2,1,0:T(1,128)}), s32[16,1,1]{2,1,0:T(1,128)S(1)}, u32[]{:S(2)}, u32[]{:S(2)}) async-start(s32[16,1,1]{2,1,0:T(1,128)} %copy.43), calls=%async_computation | async-start | bytes 16384 | tf_op jit(solution)/shard_map/all_to_all | solution.py:76
  19.5 2.3 scatter_custom_fusion
  21.8 1.1 reshape.284
  24.4 1.6 all-to-all-done
  26.0 5.3 %all-to-all-start.1 = ((bf16[16,17,1024]{2,1,0:T(8,128)(2,1)}), bf16[16,17,1024]{2,1,0:T(8,128)(2,1)S(1)}, u32[]{:S(2)}, u32[]{:S(2)}) async-start(bf16[16,17,1024]{2,1,0:T(8,128)(2,1)} %reshape.284), calls=%async_computation.1 | async-start | bytes 1572864 | tf_op jit(solution)/shard_map/all_to_all | solution.py:69
  32.7 17.8 %all-to-all-done.1 = bf16[16,17,1024]{2,1,0:T(8,128)(2,1)S(1)} async-done(((bf16[16,17,1024]{2,1,0:T(8,128)(2,1)}), bf16[16,17,1024]{2,1,0:T(8,128)(2,1)S(1)}, u32[]{:S(2)}, u32[]{:S(2)}) %all-to-all-start.1) | async-done | bytes 557088 | tf_op jit(solution)/shard_map/all_to_all | solution.py:69
  50.5 1.0 reshape.332
  51.5 2.4 scatter_custom_fusion.1
  55.1 5.5 %collective-permute-start.1 = (bf16[256,512]{1,0:T(8,128)(2,1)S(1)}, bf16[256,512]{1,0:T(8,128)(2,1)}, u32[]{:S(2)}, u32[]{:S(2)}) collective-permute-start(bf16[256,512]{1,0:T(8,128)(2,1)S(1)} %fusion.38), channel_id=1, source_target_pairs={{2,0},{4,2},{6,4},{8,6},{10,8},{12,10},{14,12},{16,14},{18,16},{20... | collective-permute-start | bytes 786440 | tf_op jit(solution)/shard_map/ppermute | solution.py:21
  60.6 2.0 convolution_convert_fusion
  62.6 0.9 copy-done.7
  63.5 1.0 reshape.365
  64.5 0.9 convert.29
  65.4 1.8 collective-permute-done.1
  67.2 2.1 convolution_convert_fusion.1
  69.4 1.3 pad_maximum_fusion
  70.6 22.5 %gather_fusion = bf16[4096,1024]{1,0:T(8,128)(2,1)} fusion(bf16[768,1024]{1,0:T(8,128)(2,1)} %pad_maximum_fusion, s32[4096]{0:T(1024)S(1)} %broadcast_clamp_fusion), kind=kCustom, calls=%fused_computation | custom fusion | bytes 16793600 | tf_op jit(solution)/shard_map/while/body/eval_jaxpr/gather | solution.py:120
  93.1 5.9 %slice_bitcast_fusion = (bf16[256,2,4,8,128]{4,3,2,1,0:T(8,128)(2,1)}, bf16[256,2,4,8,128]{4,3,2,1,0:T(8,128)(2,1)S(1)}) fusion(bf16[256,16,1024]{2,1,0:T(8,128)(2,1)} %bitcast.129), kind=kLoop, calls=%fused_computation.22 | loop fusion | bytes 16777216
  99.0 2.0 copy-done.5
  101.0 2.3 fusion.11
  104.4 1.1 copy.53
  105.5 3.5 fusion.7
  110.5 0.8 fusion.94
  111.3 0.8 copy-done.46
  112.1 1.1 fusion.18
  113.4 1.4 multiply_reduce_fusion
  115.5 1.0 reshape.367
  116.6 3.6 fusion.93
  120.2 1.3 fusion.58
  121.5 2.3 fusion.5
  124.3 2.2 copy.48
  126.9 4.4 fusion.9
  131.2 4.9 %multiply_multiply_fusion = f32[256,4,128,16]{2,1,3,0:T(4,128)S(1)} fusion(f32[256,4,16]{1,2,0:T(8,128)S(1)} %copy-done.2, f32[256,4,128]{2,1,0:T(4,128)S(1)} %copy-done.13), kind=kLoop, calls=%fused_computation.13 | loop fusion | flops 4194304 | bytes 8978432 | tf_op jit(solution)/shard_map/while/body/eval_jaxpr/mul | solution.py:205
  136.2 4.2 copy.98
  140.4 2.4 copy.49
  142.8 6.0 %broadcast_multiply_fusion = f32[256,4,128,16]{2,1,3,0:T(4,128)S(1)} fusion(f32[256,4,16]{1,2,0:T(8,128)} %copy.49, f32[256,4,128]{2,1,0:T(4,128)S(1)} %convert.31), kind=kLoop, calls=%fused_computation.24 | loop fusion | flops 2097152 | bytes 8978432 | tf_op jit(solution)/shard_map/while/body/eval_jaxpr/bhj,bhd->bjhd/dot_general | solution.py:208
  148.8 4.2 copy.97
  153.0 37.3 %scatter_custom_fusion.2 = f32[768,1024]{1,0:T(8,128)} fusion(s32[4096]{0:T(1024)} %bitcast.145, f32[4096,512]{1,0:T(8,128)} %bitcast.128, f32[]{:T(128)} %constant.147.clone.1, f32[4096,512]{1,0:T(8,128)} %bitcast.127, f32[]{:T(128)} %constant.132.clone.1), kind=kCustom, calls=%fused_computation.7 | custom fusion | flops 8388608 | bytes 19923968 | tf_op jit(solution)/shard_map/while/body/eval_jaxpr/scatter-add | solution.py:218
  190.2 2.2 convert.33
  192.5 3.5 collective-permute-start.2
  196.2 2.8 fusion.63
  199.1 8.3 %collective-permute-done.2 = bf16[256,1024]{1,0:T(8,128)(2,1)S(1)} collective-permute-done((bf16[256,1024]{1,0:T(8,128)(2,1)S(1)}, bf16[256,1024]{1,0:T(8,128)(2,1)S(1)}, u32[]{:S(2)}, u32[]{:S(2)}) %collective-permute-start.2) | collective-permute-done | bytes 524320 | tf_op jit(solution)/shard_map/ppermute | solution.py:30
  207.4 9.9 %collective-permute-done.3 = bf16[256,1024]{1,0:T(8,128)(2,1)S(1)} collective-permute-done((bf16[256,1024]{1,0:T(8,128)(2,1)S(1)}, bf16[256,1024]{1,0:T(8,128)(2,1)S(1)}, u32[]{:S(2)}, u32[]{:S(2)}) %collective-permute-start.3) | collective-permute-done | bytes 524320 | tf_op jit(solution)/shard_map/ppermute | solution.py:30
  217.3 1.5 fusion.28
  218.8 2.3 fusion.53
  221.7 3.1 fusion.20
  224.8 0.8 fusion.44
  226.0 2.1 gather_fusion.1
  228.1 1.1 reshape.294
  229.2 5.3 %all-to-all-start.2 = ((bf16[16,17,1024]{2,1,0:T(8,128)(2,1)}), bf16[16,17,1024]{2,1,0:T(8,128)(2,1)S(1)}, u32[]{:S(2)}, u32[]{:S(2)}) async-start(bf16[16,17,1024]{2,1,0:T(8,128)(2,1)} %reshape.294), calls=%async_computation.2 | async-start | bytes 1572864 | tf_op jit(solution)/shard_map/all_to_all | solution.py:266
  234.6 49.8 %all-reduce.1 = (f32[1024]{0:T(1024)S(1)}, f32[1024]{0:T(1024)S(1)}) all-reduce(f32[1024]{0:T(1024)S(1)} %pad_maximum_fusion.4, f32[1024]{0:T(1024)S(1)} %pad_maximum_fusion.5), channel_id=1, replica_groups=mesh['patch'=16,'rep'=2] {'patch','rep'}, use_global_device_ids=true, to_apply=%region_25.26 | all-reduce | flops 2048 | bytes 16384 | tf_op jit(solution)/shard_map/psum | solution.py:246
  284.6 0.8 fusion.24
  285.4 0.8 broadcast_multiply_fusion.1
  286.4 1.2 gather_fusion.2
  287.6 0.8 fusion.98
  288.4 182.0 %all-reduce.5.cloned.1.call-done = (f32[512,1536]{1,0:T(8,128)}, f32[512,512]{1,0:T(8,128)}, f32[512,2048]{1,0:T(8,128)}, f32[2048,512]{1,0:T(8,128)}) async-done(((f32[512,1536]{1,0:T(8,128)}, f32[512,512]{1,0:T(8,128)}, f32[512,2048]{1,0:T(8,128)}, f32[2048,512]{1,0:T(8,128)}), (f32[512,1536]{1,0:T(8,128)}, f32[512,512]{1,0:T(8,128)}, f32[512,2048]{1,0:T(8,128)}, ...) | async-done | bytes 12582928 | tf_op jit(solution)/shard_map/psum | solution.py:246
  470.4 3.9 copy.104
  474.3 1.0 copy.105
  475.3 2.1 copy.106
  477.4 1.6 copy-done.3
  479.0 2.1 copy.107
  481.1 1.0 copy-done.1
  (160 shorter events, 12.4 us)
Async XLA Ops:
  7.2 103.3 %copy-start = (bf16[512,2048]{1,0:T(8,128)(2,1)S(1)}, bf16[512,2048]{1,0:T(8,128)(2,1)}, u32[]{:S(2)}) copy-start(bf16[512,2048]{1,0:T(8,128)(2,1)} %param.17) | copy-start | bytes 6291460
  7.2 15.7 %copy-start.21 = (f32[32,1024]{1,0:T(8,128)S(1)}, f32[32,1024]{1,0:T(8,128)}, u32[]{:S(2)}) copy-start(f32[32,1024]{1,0:T(8,128)} %param.19) | copy-start | bytes 393220
  7.2 15.7 %copy-start.40 = (f32[32]{0:T(128)S(1)}, f32[32]{0:T(128)}, u32[]{:S(2)}) copy-start(f32[32]{0:T(128)} %param.21) | copy-start | bytes 388
  7.2 15.9 %copy-start.33 = (s32[256,16]{0,1:T(8,128)S(1)}, s32[256,16]{0,1:T(8,128)}, u32[]{:S(2)}) copy-start(s32[256,16]{0,1:T(8,128)} %param.14) | copy-start | bytes 49156
  7.2 16.1 %copy-start.23 = (f32[32,1024]{1,0:T(8,128)S(1)}, f32[32,1024]{1,0:T(8,128)}, u32[]{:S(2)}) copy-start(f32[32,1024]{1,0:T(8,128)} %param.20) | copy-start | bytes 393220
  10.4 15.5 %all-to-all-start = ((s32[16,1,1]{2,1,0:T(1,128)}), s32[16,1,1]{2,1,0:T(1,128)S(1)}, u32[]{:S(2)}, u32[]{:S(2)}) async-start(s32[16,1,1]{2,1,0:T(1,128)} %copy.43), calls=%async_computation | async-start | bytes 16384 | tf_op jit(solution)/shard_map/all_to_all | solution.py:76
  19.5 2.3 copy-start.42
  23.1 31.2 %copy-start.29 = (f32[512]{0:T(512)}, f32[512]{0:T(512)S(1)}, u32[]{:S(2)}) copy-start(f32[512]{0:T(512)S(1)} %get-tuple-element.81) | copy-start | bytes 6148
  26.0 24.5 %all-to-all-start.1 = ((bf16[16,17,1024]{2,1,0:T(8,128)(2,1)}), bf16[16,17,1024]{2,1,0:T(8,128)(2,1)S(1)}, u32[]{:S(2)}, u32[]{:S(2)}) async-start(bf16[16,17,1024]{2,1,0:T(8,128)(2,1)} %reshape.284), calls=%async_computation.1 | async-start | bytes 1572864 | tf_op jit(solution)/shard_map/all_to_all | solution.py:69
  31.3 439.1 %all-reduce.5.cloned.1.call-start = ((), (), s32[]{:S(2)}) async-start(), calls=%async_computation.3 | async-start | bytes 25165824 | tf_op jit(solution)/shard_map/psum | solution.py:246
  32.7 21.6 %copy-start.38 = (s32[272]{0:T(512)}, s32[272]{0:T(512)S(1)}, u32[]{:S(2)}) copy-start(s32[272]{0:T(512)S(1)} %fusion.84) | copy-start | bytes 3268
  54.0 1.1 copy-start.31
  54.2 0.8 copy-start.36
  54.5 10.9 %collective-permute-start = (bf16[256,512]{1,0:T(8,128)(2,1)S(1)}, bf16[256,512]{1,0:T(8,128)(2,1)}, u32[]{:S(2)}, u32[]{:S(2)}) collective-permute-start(bf16[256,512]{1,0:T(8,128)(2,1)S(1)} %fusion.38), channel_id=1, source_target_pairs={{0,2},{2,4},{4,6},{6,8},{8,10},{10,12},{12,14},{14,16},{16,18},{18... | collective-permute-start | bytes 786440 | tf_op jit(solution)/shard_map/ppermute | solution.py:19
  55.1 12.1 %collective-permute-start.1 = (bf16[256,512]{1,0:T(8,128)(2,1)S(1)}, bf16[256,512]{1,0:T(8,128)(2,1)}, u32[]{:S(2)}, u32[]{:S(2)}) collective-permute-start(bf16[256,512]{1,0:T(8,128)(2,1)S(1)} %fusion.38), channel_id=1, source_target_pairs={{2,0},{4,2},{6,4},{8,6},{10,8},{12,10},{14,12},{16,14},{18,16},{20... | collective-permute-start | bytes 786440 | tf_op jit(solution)/shard_map/ppermute | solution.py:21
  62.6 0.9 copy-start.7
  65.4 4.0 slice-start
  93.1 7.9 %copy-start.19 = (bf16[256,4,128,1]{2,3,1,0:T(2,128)(2,1)S(1)}, bf16[256,4,128,1]{2,3,1,0:T(2,128)(2,1)}, u32[]{:S(2)}) copy-start(bf16[256,4,128,1]{2,3,1,0:T(2,128)(2,1)} %reshape.365) | copy-start | bytes 786436
  99.0 2.0 copy-start.5
  103.8 0.7 copy-start.34
  105.5 4.3 copy-start.12
  109.0 1.5 copy-start.25
  109.0 1.5 copy-start.26
  109.1 0.7 copy-start.8
  110.2 4.6 copy-start.27
  110.4 4.4 copy-start.28
  110.5 1.6 copy-start.46
  112.1 1.3 copy-start.10
  113.4 1.4 copy-start.15
  114.8 1.7 copy-start.16
  116.6 3.7 copy-start.9
  116.6 5.0 %copy-start.6 = (bf16[256,2,4,8,128]{4,3,2,1,0:T(8,128)(2,1)S(1)}, bf16[256,2,4,8,128]{4,3,2,1,0:T(8,128)(2,1)}, u32[]{:S(2)}) copy-start(bf16[256,2,4,8,128]{4,3,2,1,0:T(8,128)(2,1)} %get-tuple-element.69) | copy-start | bytes 12582916
  116.6 4.9 %copy-start.20 = (bf16[256,4,128,1]{2,3,1,0:T(2,128)(2,1)S(1)}, bf16[256,4,128,1]{2,3,1,0:T(2,128)(2,1)}, u32[]{:S(2)}) copy-start(bf16[256,4,128,1]{2,3,1,0:T(2,128)(2,1)} %reshape.367) | copy-start | bytes 786436
  121.5 2.7 copy-start.35
  126.8 4.4 copy-start.2
  126.8 4.4 copy-start.13
  190.2 5.8 %copy-start.18 = (f32[256,4,1,128]{3,2,1,0:T(1,128)S(1)}, f32[256,4,1,128]{3,2,1,0:T(1,128)}, u32[]{:S(2)}) copy-start(f32[256,4,1,128]{3,2,1,0:T(1,128)} %fusion.9) | copy-start | bytes 1572868
  192.4 3.8 copy-start.11
  192.5 14.9 %collective-permute-start.2 = (bf16[256,1024]{1,0:T(8,128)(2,1)S(1)}, bf16[256,1024]{1,0:T(8,128)(2,1)S(1)}, u32[]{:S(2)}, u32[]{:S(2)}) collective-permute-start(bf16[256,1024]{1,0:T(8,128)(2,1)S(1)} %get-tuple-element.71), channel_id=1, source_target_pairs={{0,30},{2,0},{4,2},{6,4},{8,6},{10,8},{12,10},{14,12},{16,14},{18,... | collective-permute-start | bytes 1572872 | tf_op jit(solution)/shard_map/ppermute | solution.py:30
  196.0 21.2 %collective-permute-start.3 = (bf16[256,1024]{1,0:T(8,128)(2,1)S(1)}, bf16[256,1024]{1,0:T(8,128)(2,1)S(1)}, u32[]{:S(2)}, u32[]{:S(2)}) collective-permute-start(bf16[256,1024]{1,0:T(8,128)(2,1)S(1)} %get-tuple-element.72), channel_id=1, source_target_pairs={{0,2},{2,4},{4,6},{6,8},{8,10},{10,12},{12,14},{14,16},{16,18},{18... | collective-permute-start | bytes 1572872 | tf_op jit(solution)/shard_map/ppermute | solution.py:30
  221.0 0.7 copy-start.39
  221.7 3.1 copy-start.14
  221.7 3.1 copy-start.30
  221.7 3.1 copy-start.32
  221.7 3.1 copy-start.37
  228.0 6.5 %copy-start.43 = (s32[256]{0:T(256)S(1)}, s32[256]{0:T(256)}, u32[]{:S(2)}) copy-start(s32[256]{0:T(256)} %copy-done.42) | copy-start | bytes 3076
  228.1 6.5 %copy-start.44 = (f32[512]{0:T(512)S(1)}, f32[512]{0:T(512)}, u32[]{:S(2)}) copy-start(f32[512]{0:T(512)} %get-tuple-element.45) | copy-start | bytes 6148
  228.1 6.5 %copy-start.45 = (f32[512]{0:T(512)S(1)}, f32[512]{0:T(512)}, u32[]{:S(2)}) copy-start(f32[512]{0:T(512)} %get-tuple-element.57) | copy-start | bytes 6148
  228.1 56.4 %copy-start.22 = (f32[32,1024]{1,0:T(8,128)S(1)}, f32[32,1024]{1,0:T(8,128)}, u32[]{:S(2)}) copy-start(f32[32,1024]{1,0:T(8,128)} %param.19) | copy-start | bytes 393220
  228.1 56.5 %copy-start.24 = (f32[32,1024]{1,0:T(8,128)S(1)}, f32[32,1024]{1,0:T(8,128)}, u32[]{:S(2)}) copy-start(f32[32,1024]{1,0:T(8,128)} %param.20) | copy-start | bytes 393220
  228.1 57.3 %copy-start.41 = (f32[32]{0:T(128)S(1)}, f32[32]{0:T(128)}, u32[]{:S(2)}) copy-start(f32[32]{0:T(128)} %param.21) | copy-start | bytes 388
  229.2 57.0 %all-to-all-start.2 = ((bf16[16,17,1024]{2,1,0:T(8,128)(2,1)}), bf16[16,17,1024]{2,1,0:T(8,128)(2,1)S(1)}, u32[]{:S(2)}, u32[]{:S(2)}) async-start(bf16[16,17,1024]{2,1,0:T(8,128)(2,1)} %reshape.294), calls=%async_computation.2 | async-start | bytes 1572864 | tf_op jit(solution)/shard_map/all_to_all | solution.py:266
  470.4 3.9 copy-start.17
  470.4 4.9 copy-start.4
  475.3 3.7 copy-start.3
  479.0 3.1 copy-start.1
Sparse Core Ops, SparseCore 0:
  221.2 249.1 all-reduce.4
where the time goes:
time: 494 us; the launch traced here: 489 us
  waiting for transfers between devices  221 us (45%)
  local copies, waits for them, and re-layouts  74.2 us (15%)
  other arithmetic  64.3 us (13%)
  blocking collectives  49.8 us (10%)
  matrix products  35.6 us (7%)
  starting transfers between devices  28.7 us (6%)
  between operations  15.1 us (3%)
    psum x1, waiting for transfers between devices, local(): lax.psum((gradient_proj, gradient_out, gradient_up, gradient_down, coeff_...  182 us
    psum x1, blocking collectives, local(): lax.psum((gradient_proj, gradient_out, gradient_up, gradient_down, coeff_...  49.8 us
    scatter-add x1, other arithmetic, backward_block(): table_grad = table_grad.at[index_block.reshape(-1)].add(pair_grad)  37.3 us
    unnamed x102, local copies, waits for them, and re-layouts  31.4 us
    gather x1, local copies, waits for them, and re-layouts, gather_block(): gathered = kv_table[index_block]  22.5 us
    ppermute x2, waiting for transfers between devices, from_behind(): lax.ppermute(array, axis, [(i, (i + by) % size) for i in range(size)])  18.2 us
    all_to_all x1, waiting for transfers between devices, local(): lax.all_to_all(outgoing.reshape(patch_count, capacity, 2 * feature_width)...  17.8 us
  transfers between devices with their start and end apart: 8, of which 6 were waited for; matrix products, arithmetic and copies ran while one was open for 5% of the time, Pallas kernels for 0%

commit v1 on v0

--- a/solution.py
+++ b/solution.py
@@ -7,6 +7,17 @@
 HD = 128
 NEIGH = 16
 NORM_EPS = 1e-05
+
+
+def bench_render(block_here, at_axis, view):
+    upper, shaped = (block_here.shape[:at_axis], block_here.shape[at_axis + 1 :])
+    return jnp.moveaxis(block_here.reshape(*upper, view, -1, *shaped), at_axis, 0)
+
+
+def samples_remake(local_block, ndim_at):
+    t1 = list(local_block.shape[1:])
+    t1[ndim_at] *= local_block.shape[0]
+    return jnp.moveaxis(local_block, 0, ndim_at).reshape(t1)
 
 
 def extended(cells, sides, width):
@@ -65,6 +76,23 @@
     flat_slot = dest * capacity + slot_index
     outgoing = jnp.zeros((patch_count * capacity, 2 * feature_width), jnp.bfloat16)
     outgoing = outgoing.at[flat_slot].set(jnp.concatenate([tokens, cotangent], axis=1))
+
+    def press_axis_part(frame, group_axis, patch, piece_in):
+        mid_arr, piece_next = (jax.lax.axis_size(group_axis), jax.lax.axis_index(group_axis))
+        spare = bench_render(frame, patch, mid_arr)
+        series = [spare[piece_next]]
+        c = 1
+        while c < mid_arr:
+            local_next = spare[piece_next ^ c]
+            series.append(
+                jax.lax.ppermute(
+                    local_next, axis_name=group_axis, perm=[(u, u ^ c) for u in range(mid_arr)]
+                )
+            )
+            c += 1
+        spare = jnp.stack(series, axis=0)[piece_next ^ jnp.arange(mid_arr)]
+        return samples_remake(spare, piece_in)
+
     arrived, arrived_counts = (
         lax.all_to_all(
             outgoing.reshape(patch_count, capacity, 2 * feature_width),
@@ -73,7 +101,7 @@
             concat_axis=0,
             tiled=True,
         ),
-        lax.all_to_all(sent_counts[:, None], "patch", split_axis=0, concat_axis=0, tiled=True),
+        press_axis_part(sent_counts[:, None], "patch", 0, 0),
     )
     counts_in = arrived_counts[:, 0]
     offsets = jnp.cumsum(counts_in) - counts_in

time: 494 us -> 511 us (1.034)
  starting transfers between devices: 28.7 us -> 50.3 us
  waiting for transfers between devices: 221 us -> 205 us
  local copies, waits for them, and re-layouts: 74.2 us -> 85.1 us
    ppermute x0 -> x15, starting transfers between devices: none -> 29.7 us  [press_axis_part(): jax.lax.ppermute(local_next, axis_name=group_axis, perm=[(u, u ^ c) for u...]
    all_to_all x1, waiting for transfers between devices: 17.8 us -> 0.01 us  [local(): lax.all_to_all(outgoing.reshape(patch_count, capacity, 2 * feature_width)...]
    another operation x4 -> x6, local copies, waits for them, and re-layouts: 4.77 us -> 14.9 us  [the longest x1 10.1 us: press_axis_part(): spare = jnp.stack(series, axis=0)[piece_next ^ jnp.arange(mid_arr)]]
    all_to_all x1 -> x0, starting transfers between devices: 8.31 us -> none  [local(): lax.all_to_all(sent_counts[:, None], 'patch', split_axis=0, concat_axis=0...]
    ppermute x0 -> x15, waiting for transfers between devices: none -> 7.08 us  [press_axis_part(): jax.lax.ppermute(local_next, axis_name=group_axis, perm=[(u, u ^ c) for u...]
  transfers between devices with their start and end apart: 8 -> 22, of which waited for: 6 -> 7; matrix products, arithmetic and copies ran while one was open for 5% -> 7% of each run, Pallas kernels for 0% -> 0%
where the time goes in v1:
time: 511 us; the launch traced here: 505 us
  waiting for transfers between devices  205 us (40%)
  local copies, waits for them, and re-layouts  85.1 us (17%)
  other arithmetic  63.9 us (13%)
  starting transfers between devices  50.3 us (10%)
  blocking collectives  49.6 us (10%)
  matrix products  35.7 us (7%)
  between operations  15.3 us (3%)
    psum x1, waiting for transfers between devices, local(): lax.psum((gradient_proj, gradient_out, gradient_up, gradient_down, coeff_...  182 us
    psum x1, blocking collectives, local(): lax.psum((gradient_proj, gradient_out, gradient_up, gradient_down, coeff_...  49.6 us
    scatter-add x1, other arithmetic, backward_block(): table_grad = table_grad.at[index_block.reshape(-1)].add(pair_grad)  37.3 us
    unnamed x102, local copies, waits for them, and re-layouts  31.5 us
    ppermute x15, starting transfers between devices, press_axis_part(): jax.lax.ppermute(local_next, axis_name=group_axis, perm=[(u, u ^ c) for u...  29.7 us
    gather x1, local copies, waits for them, and re-layouts, gather_block(): gathered = kv_table[index_block]  22.5 us
    ppermute x2, waiting for transfers between devices, from_behind(): lax.ppermute(array, axis, [(i, (i + by) % size) for i in range(size)])  15.1 us
  transfers between devices with their start and end apart: 22, of which 7 were waited for; matrix products, arithmetic and copies ran while one was open for 7% of the time, Pallas kernels for 0%

profile of v1, /device:TPU:0, one launch (start us, length us, event | category | flops | bytes accessed | tf_op | source)
XLA Modules:
  0.0 505.3 jit_solution(8094810165436750093)
XLA Ops:
  10.7 4.0 collective-permute-start.4
  14.6 1.4 collective-permute-start.5
  16.1 1.5 collective-permute-start.6
  17.5 2.6 collective-permute-start.7
  20.1 1.3 collective-permute-start.8
  22.1 2.3 scatter_custom_fusion
  24.4 1.1 reshape.329
  25.5 4.9 all-to-all-start
  32.6 1.9 collective-permute-start
  34.6 3.3 collective-permute-start.9
  37.9 3.7 collective-permute-start.11
  41.7 1.5 collective-permute-start.12
  43.1 4.2 collective-permute-start.13
  47.3 2.8 collective-permute-done.9
  50.1 2.3 collective-permute-start.14
  52.4 1.5 collective-permute-start.1
  54.5 2.9 collective-permute-done.14
  57.4 1.4 collective-permute-done.2
  58.7 10.1 %stack.63 = s32[16,1,1]{0,2,1:T(1,128)S(1)} concatenate(s32[1,1,1]{0,2,1:T(1,128)} %bitcast, s32[1,1,1]{0,2,1:T(1,128)} %bitcast.2, s32[1,1,1]{0,2,1:T(1,128)} %bitcast.4, s32[1,1,1]{0,2,1:T(1,128)} %bitcast.6, s32[1,1,1]{0,2,1:T(1,128)} %bitcast.8, s32[1,1,1]{0,2,1:T(1,128)} %bitcast.10, s32[1,1,1]{0,2,1:T(1,128)} %bitcast.12, s32[1,1,1]{0,2,1:T(1,128)} %bitcast.14, ...), dimensions={0} | concatenate | bytes 128 | tf_op jit(solution)/shard_map/stack | solution.py:93
  69.9 1.0 reshape.389
  70.9 2.4 scatter_custom_fusion.1
  73.9 1.0 collective-permute-start.15
  74.9 5.1 %collective-permute-start.16 = (bf16[256,512]{1,0:T(8,128)(2,1)S(1)}, bf16[256,512]{1,0:T(8,128)(2,1)}, u32[]{:S(2)}, u32[]{:S(2)}) collective-permute-start(bf16[256,512]{1,0:T(8,128)(2,1)S(1)} %fusion.38), channel_id=1, source_target_pairs={{2,0},{4,2},{6,4},{8,6},{10,8},{12,10},{14,12},{16,14},{18,16},{20... | collective-permute-start | bytes 786440 | tf_op jit(solution)/shard_map/ppermute | solution.py:32
  80.0 2.0 convolution_convert_fusion
  85.5 2.1 convolution_convert_fusion.1
  87.7 1.3 pad_maximum_fusion
  89.0 22.5 %gather_fusion.1 = bf16[4096,1024]{1,0:T(8,128)(2,1)} fusion(bf16[768,1024]{1,0:T(8,128)(2,1)} %pad_maximum_fusion, s32[4096]{0:T(1024)S(1)} %broadcast_clamp_fusion), kind=kCustom, calls=%fused_computation.1 | custom fusion | bytes 16793600 | tf_op jit(solution)/shard_map/while/body/eval_jaxpr/gather | solution.py:148
  111.5 5.9 %slice_bitcast_fusion = (bf16[256,2,4,8,128]{4,3,2,1,0:T(8,128)(2,1)}, bf16[256,2,4,8,128]{4,3,2,1,0:T(8,128)(2,1)S(1)}) fusion(bf16[256,16,1024]{2,1,0:T(8,128)(2,1)} %bitcast.163), kind=kLoop, calls=%fused_computation.23 | loop fusion | bytes 16777216
  117.3 2.0 copy-done.5
  119.4 2.3 fusion.11
  122.8 1.1 copy.38
  123.9 3.5 fusion.7
  130.4 1.1 fusion.18
  131.7 1.4 multiply_reduce_fusion
  133.8 1.0 reshape.428
  135.0 3.7 fusion.94
  138.6 1.3 fusion.58
  139.9 2.3 fusion.5
  142.7 2.2 copy.33
  145.2 4.4 fusion.9
  149.6 4.9 multiply_multiply_fusion
  154.5 4.2 copy.83
  158.8 2.4 copy.34
  161.2 6.0 %broadcast_multiply_fusion = f32[256,4,128,16]{2,1,3,0:T(4,128)S(1)} fusion(f32[256,4,16]{1,2,0:T(8,128)} %copy.34, f32[256,4,128]{2,1,0:T(4,128)S(1)} %convert.31), kind=kLoop, calls=%fused_computation.25 | loop fusion | flops 2097152 | bytes 8978432 | tf_op jit(solution)/shard_map/while/body/eval_jaxpr/bhj,bhd->bjhd/dot_general | solution.py:236
  167.2 4.2 copy.82
  171.4 37.3 %scatter_custom_fusion.2 = f32[768,1024]{1,0:T(8,128)} fusion(s32[4096]{0:T(1024)} %bitcast.178, f32[4096,512]{1,0:T(8,128)} %bitcast.162, f32[]{:T(128)} %constant.191.clone.1, f32[4096,512]{1,0:T(8,128)} %bitcast.161, f32[]{:T(128)} %constant.182.clone.1), kind=kCustom, calls=%fused_computation.8 | custom fusion | flops 8388608 | bytes 19923968 | tf_op jit(solution)/shard_map/while/body/eval_jaxpr/scatter-add | solution.py:246
  208.6 2.2 convert.33
  210.9 4.6 collective-permute-start.17
  215.7 2.8 fusion.63
  218.5 7.3 %collective-permute-done.17 = bf16[256,1024]{1,0:T(8,128)(2,1)S(1)} collective-permute-done((bf16[256,1024]{1,0:T(8,128)(2,1)S(1)}, bf16[256,1024]{1,0:T(8,128)(2,1)S(1)}, u32[]{:S(2)}, u32[]{:S(2)}) %collective-permute-start.17) | collective-permute-done | bytes 524320 | tf_op jit(solution)/shard_map/ppermute | solution.py:41
  225.8 7.8 %collective-permute-done.18 = bf16[256,1024]{1,0:T(8,128)(2,1)S(1)} collective-permute-done((bf16[256,1024]{1,0:T(8,128)(2,1)S(1)}, bf16[256,1024]{1,0:T(8,128)(2,1)S(1)}, u32[]{:S(2)}, u32[]{:S(2)}) %collective-permute-start.18) | collective-permute-done | bytes 524320 | tf_op jit(solution)/shard_map/ppermute | solution.py:41
  233.6 1.5 fusion.28
  235.1 2.3 fusion.53
  238.0 3.1 fusion.20
  242.3 2.1 gather_fusion.2
  244.4 1.1 reshape.339
  245.5 4.9 all-to-all-start.1
  250.5 49.6 %all-reduce.1 = (f32[1024]{0:T(1024)S(1)}, f32[1024]{0:T(1024)S(1)}) all-reduce(f32[1024]{0:T(1024)S(1)} %pad_maximum_fusion.4, f32[1024]{0:T(1024)S(1)} %pad_maximum_fusion.5), channel_id=1, replica_groups=mesh['patch'=16,'rep'=2] {'patch','rep'}, use_global_device_ids=true, to_apply=%region_25.26 | all-reduce | flops 2048 | bytes 16384 | tf_op jit(solution)/shard_map/psum | solution.py:274
  302.1 1.2 gather_fusion.3
  304.1 182.5 %all-reduce.5.cloned.1.call-done = (f32[512,1536]{1,0:T(8,128)}, f32[512,512]{1,0:T(8,128)}, f32[512,2048]{1,0:T(8,128)}, f32[2048,512]{1,0:T(8,128)}) async-done(((f32[512,1536]{1,0:T(8,128)}, f32[512,512]{1,0:T(8,128)}, f32[512,2048]{1,0:T(8,128)}, f32[2048,512]{1,0:T(8,128)}), (f32[512,1536]{1,0:T(8,128)}, f32[512,512]{1,0:T(8,128)}, f32[512,2048]{1,0:T(8,128)}, ...) | async-done | bytes 12582928 | tf_op jit(solution)/shard_map/psum | solution.py:274
  486.5 3.9 copy.89
  491.4 2.1 copy.91
  493.5 1.6 copy-done.3
  495.1 2.1 copy.92
  (192 shorter events, 24.7 us)
Async XLA Ops:
  7.2 121.6 %copy-start = (bf16[512,2048]{1,0:T(8,128)(2,1)S(1)}, bf16[512,2048]{1,0:T(8,128)(2,1)}, u32[]{:S(2)}) copy-start(bf16[512,2048]{1,0:T(8,128)(2,1)} %param.17) | copy-start | bytes 6291460
  7.3 23.2 %copy-start.21 = (f32[32,1024]{1,0:T(8,128)S(1)}, f32[32,1024]{1,0:T(8,128)}, u32[]{:S(2)}) copy-start(f32[32,1024]{1,0:T(8,128)} %param.19) | copy-start | bytes 393220
  7.3 23.2 %copy-start.40 = (f32[32]{0:T(128)S(1)}, f32[32]{0:T(128)}, u32[]{:S(2)}) copy-start(f32[32]{0:T(128)} %param.21) | copy-start | bytes 388
  9.9 20.8 %copy-start.33 = (s32[256,16]{0,1:T(8,128)S(1)}, s32[256,16]{0,1:T(8,128)}, u32[]{:S(2)}) copy-start(s32[256,16]{0,1:T(8,128)} %param.14) | copy-start | bytes 49156
  10.7 22.0 %collective-permute-start.4 = (s32[1,1]{1,0:T(1,128)}, s32[1,1]{1,0:T(1,128)}, u32[]{:S(2)}, u32[]{:S(2)}) collective-permute-start(s32[1,1]{1,0:T(1,128)} %bitcast.9), channel_id=1, source_target_pairs={{0,10},{2,8},{4,14},{6,12},{8,2},{10,0},{12,6},{14,4},{16,26},{18,... | collective-permute-start | bytes 20 | tf_op jit(solution)/shard_map/ppermute | solution.py:88
  14.6 19.9 %collective-permute-start.5 = (s32[1,1]{1,0:T(1,128)}, s32[1,1]{1,0:T(1,128)}, u32[]{:S(2)}, u32[]{:S(2)}) collective-permute-start(s32[1,1]{1,0:T(1,128)} %bitcast.11), channel_id=1, source_target_pairs={{0,12},{2,14},{4,8},{6,10},{8,4},{10,6},{12,0},{14,2},{16,28},{18,... | collective-permute-start | bytes 20 | tf_op jit(solution)/shard_map/ppermute | solution.py:88
  16.1 21.8 %collective-permute-start.6 = (s32[1,1]{1,0:T(1,128)}, s32[1,1]{1,0:T(1,128)}, u32[]{:S(2)}, u32[]{:S(2)}) collective-permute-start(s32[1,1]{1,0:T(1,128)} %bitcast.13), channel_id=1, source_target_pairs={{0,14},{2,12},{4,10},{6,8},{8,6},{10,4},{12,2},{14,0},{16,30},{18,... | collective-permute-start | bytes 20 | tf_op jit(solution)/shard_map/ppermute | solution.py:88
  17.5 20.4 %collective-permute-start.7 = (s32[1,1]{1,0:T(1,128)}, s32[1,1]{1,0:T(1,128)}, u32[]{:S(2)}, u32[]{:S(2)}) collective-permute-start(s32[1,1]{1,0:T(1,128)} %bitcast.15), channel_id=1, source_target_pairs={{0,16},{2,18},{4,20},{6,22},{8,24},{10,26},{12,28},{14,30},{16,0},... | collective-permute-start | bytes 20 | tf_op jit(solution)/shard_map/ppermute | solution.py:88
  20.1 21.5 %collective-permute-start.8 = (s32[1,1]{1,0:T(1,128)}, s32[1,1]{1,0:T(1,128)}, u32[]{:S(2)}, u32[]{:S(2)}) collective-permute-start(s32[1,1]{1,0:T(1,128)} %bitcast.17), channel_id=1, source_target_pairs={{0,18},{2,16},{4,22},{6,20},{8,26},{10,24},{12,30},{14,28},{16,2},... | collective-permute-start | bytes 20 | tf_op jit(solution)/shard_map/ppermute | solution.py:88
  22.1 8.4 %copy-start.42 = (s32[256]{0:T(256)}, s32[256]{0:T(256)S(1)}, u32[]{:S(2)}) copy-start(s32[256]{0:T(256)S(1)} %compare_select_fusion.3) | copy-start | bytes 3076
  22.1 8.9 %copy-start.23 = (f32[32,1024]{1,0:T(8,128)S(1)}, f32[32,1024]{1,0:T(8,128)}, u32[]{:S(2)}) copy-start(f32[32,1024]{1,0:T(8,128)} %param.20) | copy-start | bytes 393220
  25.5 44.5 %all-to-all-start = ((bf16[16,17,1024]{2,1,0:T(8,128)(2,1)}), bf16[16,17,1024]{2,1,0:T(8,128)(2,1)S(1)}, u32[]{:S(2)}, u32[]{:S(2)}) async-start(bf16[16,17,1024]{2,1,0:T(8,128)(2,1)} %reshape.329), calls=%async_computation | async-start | bytes 1572864 | tf_op jit(solution)/shard_map/all_to_all | solution.py:97
  30.4 456.1 %all-reduce.5.cloned.1.call-start = ((), (), s32[]{:S(2)}) async-start(), calls=%async_computation.2 | async-start | bytes 25165824 | tf_op jit(solution)/shard_map/psum | solution.py:274
  30.7 43.2 %copy-start.29 = (f32[512]{0:T(512)}, f32[512]{0:T(512)S(1)}, u32[]{:S(2)}) copy-start(f32[512]{0:T(512)S(1)} %get-tuple-element.81) | copy-start | bytes 6148
  32.6 10.5 %collective-permute-start = (s32[1,1]{1,0:T(1,128)}, s32[1,1]{1,0:T(1,128)}, u32[]{:S(2)}, u32[]{:S(2)}) collective-permute-start(s32[1,1]{1,0:T(1,128)} %bitcast.1), channel_id=1, source_target_pairs={{0,2},{2,0},{4,6},{6,4},{8,10},{10,8},{12,14},{14,12},{16,18},{18,... | collective-permute-start | bytes 20 | tf_op jit(solution)/shard_map/ppermute | solution.py:88
  34.6 15.6 %collective-permute-start.9 = (s32[1,1]{1,0:T(1,128)}, s32[1,1]{1,0:T(1,128)}, u32[]{:S(2)}, u32[]{:S(2)}) collective-permute-start(s32[1,1]{1,0:T(1,128)} %bitcast.19), channel_id=1, source_target_pairs={{0,20},{2,22},{4,16},{6,18},{8,28},{10,30},{12,24},{14,26},{16,4},... | collective-permute-start | bytes 20 | tf_op jit(solution)/shard_map/ppermute | solution.py:88
  37.8 14.6 %collective-permute-start.10 = (s32[1,1]{1,0:T(1,128)}, s32[1,1]{1,0:T(1,128)}, u32[]{:S(2)}, u32[]{:S(2)}) collective-permute-start(s32[1,1]{1,0:T(1,128)} %bitcast.21), channel_id=1, source_target_pairs={{0,22},{2,20},{4,18},{6,16},{8,30},{10,28},{12,26},{14,24},{16,6},... | collective-permute-start | bytes 20 | tf_op jit(solution)/shard_map/ppermute | solution.py:88
  37.9 16.0 %collective-permute-start.11 = (s32[1,1]{1,0:T(1,128)}, s32[1,1]{1,0:T(1,128)}, u32[]{:S(2)}, u32[]{:S(2)}) collective-permute-start(s32[1,1]{1,0:T(1,128)} %bitcast.23), channel_id=1, source_target_pairs={{0,24},{2,26},{4,28},{6,30},{8,16},{10,18},{12,20},{14,22},{16,8},... | collective-permute-start | bytes 20 | tf_op jit(solution)/shard_map/ppermute | solution.py:88
  41.7 12.8 %collective-permute-start.12 = (s32[1,1]{1,0:T(1,128)}, s32[1,1]{1,0:T(1,128)}, u32[]{:S(2)}, u32[]{:S(2)}) collective-permute-start(s32[1,1]{1,0:T(1,128)} %bitcast.25), channel_id=1, source_target_pairs={{0,26},{2,24},{4,30},{6,28},{8,18},{10,16},{12,22},{14,20},{16,10}... | collective-permute-start | bytes 20 | tf_op jit(solution)/shard_map/ppermute | solution.py:88
  43.1 11.3 %collective-permute-start.13 = (s32[1,1]{1,0:T(1,128)}, s32[1,1]{1,0:T(1,128)}, u32[]{:S(2)}, u32[]{:S(2)}) collective-permute-start(s32[1,1]{1,0:T(1,128)} %bitcast.27), channel_id=1, source_target_pairs={{0,28},{2,30},{4,24},{6,26},{8,20},{10,22},{12,16},{14,18},{16,12}... | collective-permute-start | bytes 20 | tf_op jit(solution)/shard_map/ppermute | solution.py:88
  50.1 7.2 %collective-permute-start.14 = (s32[1,1]{1,0:T(1,128)}, s32[1,1]{1,0:T(1,128)}, u32[]{:S(2)}, u32[]{:S(2)}) collective-permute-start(s32[1,1]{1,0:T(1,128)} %bitcast.29), channel_id=1, source_target_pairs={{0,30},{2,28},{4,26},{6,24},{8,22},{10,20},{12,18},{14,16},{16,14}... | collective-permute-start | bytes 20 | tf_op jit(solution)/shard_map/ppermute | solution.py:88
  52.4 4.9 collective-permute-start.1
  53.9 4.8 collective-permute-start.2
  54.5 4.2 collective-permute-start.3
  69.9 12.1 %copy-start.38 = (s32[272]{0:T(512)}, s32[272]{0:T(512)S(1)}, u32[]{:S(2)}) copy-start(s32[272]{0:T(512)S(1)} %fusion.84) | copy-start | bytes 3268
  73.4 1.4 copy-start.31
  73.9 10.9 %collective-permute-start.15 = (bf16[256,512]{1,0:T(8,128)(2,1)S(1)}, bf16[256,512]{1,0:T(8,128)(2,1)}, u32[]{:S(2)}, u32[]{:S(2)}) collective-permute-start(bf16[256,512]{1,0:T(8,128)(2,1)S(1)} %fusion.38), channel_id=1, source_target_pairs={{0,2},{2,4},{4,6},{6,8},{8,10},{10,12},{12,14},{14,16},{16,18},{18... | collective-permute-start | bytes 786440 | tf_op jit(solution)/shard_map/ppermute | solution.py:30
  74.9 10.7 %collective-permute-start.16 = (bf16[256,512]{1,0:T(8,128)(2,1)S(1)}, bf16[256,512]{1,0:T(8,128)(2,1)}, u32[]{:S(2)}, u32[]{:S(2)}) collective-permute-start(bf16[256,512]{1,0:T(8,128)(2,1)S(1)} %fusion.38), channel_id=1, source_target_pairs={{2,0},{4,2},{6,4},{8,6},{10,8},{12,10},{14,12},{16,14},{18,16},{20... | collective-permute-start | bytes 786440 | tf_op jit(solution)/shard_map/ppermute | solution.py:32
  84.8 3.0 slice-start
  111.5 7.9 %copy-start.19 = (bf16[256,4,128,1]{2,3,1,0:T(2,128)(2,1)S(1)}, bf16[256,4,128,1]{2,3,1,0:T(2,128)(2,1)}, u32[]{:S(2)}) copy-start(bf16[256,4,128,1]{2,3,1,0:T(2,128)(2,1)} %reshape.426) | copy-start | bytes 786436
  117.3 2.0 copy-start.5
  123.9 4.3 copy-start.12
  127.3 1.5 copy-start.25
  127.3 1.5 copy-start.26
  128.6 4.6 copy-start.27
  128.8 4.4 copy-start.28
  128.8 1.6 copy-start.46
  131.7 1.4 copy-start.15
  133.2 1.7 copy-start.16
  134.9 3.7 copy-start.9
  134.9 5.0 copy-start.6
  135.0 5.0 copy-start.20
  139.9 2.7 copy-start.35
  145.2 4.4 copy-start.2
  145.2 4.4 copy-start.13
  208.6 6.9 %copy-start.18 = (f32[256,4,1,128]{3,2,1,0:T(1,128)S(1)}, f32[256,4,1,128]{3,2,1,0:T(1,128)}, u32[]{:S(2)}) copy-start(f32[256,4,1,128]{3,2,1,0:T(1,128)} %fusion.9) | copy-start | bytes 1572868
  210.8 4.9 copy-start.11
  210.9 14.9 %collective-permute-start.17 = (bf16[256,1024]{1,0:T(8,128)(2,1)S(1)}, bf16[256,1024]{1,0:T(8,128)(2,1)S(1)}, u32[]{:S(2)}, u32[]{:S(2)}) collective-permute-start(bf16[256,1024]{1,0:T(8,128)(2,1)S(1)} %get-tuple-element.71), channel_id=1, source_target_pairs={{0,30},{2,0},{4,2},{6,4},{8,6},{10,8},{12,10},{14,12},{16,14},{18,... | collective-permute-start | bytes 1572872 | tf_op jit(solution)/shard_map/ppermute | solution.py:41
  215.5 18.1 %collective-permute-start.18 = (bf16[256,1024]{1,0:T(8,128)(2,1)S(1)}, bf16[256,1024]{1,0:T(8,128)(2,1)S(1)}, u32[]{:S(2)}, u32[]{:S(2)}) collective-permute-start(bf16[256,1024]{1,0:T(8,128)(2,1)S(1)} %get-tuple-element.72), channel_id=1, source_target_pairs={{0,2},{2,4},{4,6},{6,8},{8,10},{10,12},{12,14},{14,16},{16,18},{18... | collective-permute-start | bytes 1572872 | tf_op jit(solution)/shard_map/ppermute | solution.py:41
  238.0 3.1 copy-start.14
  238.0 3.1 copy-start.30
  238.0 3.1 copy-start.32
  238.0 3.1 copy-start.37
  244.4 6.1 %copy-start.43 = (s32[256]{0:T(256)S(1)}, s32[256]{0:T(256)}, u32[]{:S(2)}) copy-start(s32[256]{0:T(256)} %copy-done.42) | copy-start | bytes 3076
  244.4 6.1 %copy-start.44 = (f32[512]{0:T(512)S(1)}, f32[512]{0:T(512)}, u32[]{:S(2)}) copy-start(f32[512]{0:T(512)} %get-tuple-element.45) | copy-start | bytes 6148
  244.4 6.1 %copy-start.45 = (f32[512]{0:T(512)S(1)}, f32[512]{0:T(512)}, u32[]{:S(2)}) copy-start(f32[512]{0:T(512)} %get-tuple-element.57) | copy-start | bytes 6148
  244.4 55.7 %copy-start.22 = (f32[32,1024]{1,0:T(8,128)S(1)}, f32[32,1024]{1,0:T(8,128)}, u32[]{:S(2)}) copy-start(f32[32,1024]{1,0:T(8,128)} %param.19) | copy-start | bytes 393220
  244.4 55.9 %copy-start.24 = (f32[32,1024]{1,0:T(8,128)S(1)}, f32[32,1024]{1,0:T(8,128)}, u32[]{:S(2)}) copy-start(f32[32,1024]{1,0:T(8,128)} %param.20) | copy-start | bytes 393220
  244.4 56.6 %copy-start.41 = (f32[32]{0:T(128)S(1)}, f32[32]{0:T(128)}, u32[]{:S(2)}) copy-start(f32[32]{0:T(128)} %param.21) | copy-start | bytes 388
  245.5 56.3 %all-to-all-start.1 = ((bf16[16,17,1024]{2,1,0:T(8,128)(2,1)}), bf16[16,17,1024]{2,1,0:T(8,128)(2,1)S(1)}, u32[]{:S(2)}, u32[]{:S(2)}) async-start(bf16[16,17,1024]{2,1,0:T(8,128)(2,1)} %reshape.339), calls=%async_computation.1 | async-start | bytes 1572864 | tf_op jit(solution)/shard_map/all_to_all | solution.py:294
  486.5 3.9 copy-start.17
  486.5 4.9 copy-start.4
  491.4 3.7 copy-start.3
  495.1 3.1 copy-start.1
  (6 other events, 5.4 us)
Sparse Core Ops, SparseCore 0:
  237.5 248.9 all-reduce.4
